TPU v7x, 256 devices: a whole 4x4x8 slice. The times are simulated.
256 devices in a mesh: expert: 128 (over y, x, z), dp: 2 (over core).
Axes of the slice: x: 4, y: 4, z: 8, core: 2. Of those that a mesh axis runs over, the one named last changes fastest.
Arguments:
- tokens: bfloat16 [4096, 2048], P(('dp', 'expert')), parts along dimension 0, may hold values from -6 to 6
- expert_ids: int32 [4096, 8], P(('dp', 'expert')), parts along dimension 0, may hold values from 0 to 127, all different within a row; in each aligned block of 16 rows (0 to 15, 16 to 31, ...) at most 2 rows name the same one
- gate_values: float32 [4096, 8], P(('dp', 'expert')), parts along dimension 0, may hold values from 0.03 to 0.4
- w_gate: bfloat16 [128, 2048, 768], P('expert'), may hold values from -0.125 to 0.125
- w_up: bfloat16 [128, 2048, 768], P('expert'), may hold values from -0.125 to 0.125
- w_down: bfloat16 [128, 768, 2048], P('expert'), may hold values from -0.21875 to 0.21875
- cotangent: bfloat16 [4096, 2048], P(('dp', 'expert')), parts along dimension 0, may hold values from -6 to 6
Outputs:
- mixed_rows: bfloat16 [4096, 2048], P(('dp', 'expert')), parts along dimension 0
- row_grads: bfloat16 [4096, 2048], P(('dp', 'expert')), parts along dimension 0
- gate_grads: float32 [4096, 8], P(('dp', 'expert')), parts along dimension 0
There are 2 independent parts, one for each index of `dp`. A program takes and returns all parts, laid end to end along the dimension named above; an argument that names none is the same for every part. Nothing has to cross between parts.
Inputs may be any that keep to these rules, and one draw needn't show every extreme that they name: `expert_ids`: each token names 8 different experts. Among the 16 tokens of one device no expert is named more than 2 times, and in every draw some device names some expert exactly 2 times.
All inputs are finite; a program needn't handle non-finite values.
Results may differ from a plain program's by a relative error of at most 0.0064.
Values may be sent and summed in bfloat16 or wider, within the bound.
No kernel may reach another device: no remote copies, remote signals or barrier semaphores. Data moves between devices by JAX's collectives and lax.ppermute only.
A program may use at most 128 MiB of HBM per device.

v0:
```python
import jax
import jax.numpy as jnp
from jax import lax
from jax.sharding import PartitionSpec as P


def expert_forward(inputs, gate_matrix, up_matrix, down_matrix):
    pre_gate = jnp.dot(inputs, gate_matrix, preferred_element_type=jnp.float32)
    pre_up = jnp.dot(inputs, up_matrix, preferred_element_type=jnp.float32)
    hidden = (pre_gate * jax.nn.sigmoid(pre_gate) * pre_up).astype(jnp.bfloat16)
    output = jnp.dot(hidden, down_matrix, preferred_element_type=jnp.float32).astype(jnp.bfloat16)
    return (output, pre_gate, pre_up)


def expert_backward(grad_output, pre_gate, pre_up, gate_matrix, up_matrix, down_matrix):
    contract = (((1,), (1,)), ((), ()))
    grad_hidden = lax.dot_general(
        grad_output, down_matrix, contract, preferred_element_type=jnp.float32
    )
    sigmoid = jax.nn.sigmoid(pre_gate)
    grad_gate = (grad_hidden * pre_up * sigmoid * (1.0 + pre_gate * (1.0 - sigmoid))).astype(
        jnp.bfloat16
    )
    grad_up = (grad_hidden * pre_gate * sigmoid).astype(jnp.bfloat16)
    first_part = lax.dot_general(
        grad_gate, gate_matrix, contract, preferred_element_type=jnp.float32
    )
    second_part = lax.dot_general(grad_up, up_matrix, contract, preferred_element_type=jnp.float32)
    return (first_part + second_part).astype(jnp.bfloat16)


def slot_places(expert_ids, experts, capacity):
    flat_ids = expert_ids.reshape(-1)
    matches = (flat_ids[:, None] == jnp.arange(experts, dtype=jnp.int32)[None, :]).astype(jnp.int32)
    ranked = jnp.sum((jnp.cumsum(matches, axis=0) - matches) * matches, axis=1)
    return flat_ids * capacity + ranked


def local(tokens, expert_ids, gate_values, w_gate, w_up, w_down, cotangent):
    row_count, model_width = tokens.shape
    top_count = expert_ids.shape[1]
    experts = lax.axis_size("expert")
    capacity = max(2, 2 * row_count * top_count // experts)
    slot_total = experts * capacity
    entry_count = row_count * top_count
    gate_matrix = w_gate[0]
    up_matrix = w_up[0]
    down_matrix = w_down[0]
    places = slot_places(expert_ids, experts, capacity)
    flat_gates = gate_values.reshape(-1)
    upstream = jnp.repeat(cotangent, top_count, axis=0)
    padding = jnp.zeros((1, model_width), jnp.bfloat16)
    gathered_ids = lax.all_gather(expert_ids, "expert", axis=0, tiled=True)
    all_gates = lax.all_gather(gate_values, "expert", axis=0, tiled=True)
    all_tokens, all_cotangent = (
        lax.all_gather(tokens, "expert", axis=0, tiled=True),
        lax.all_gather(cotangent, "expert", axis=0, tiled=True),
    )
    own_expert = lax.axis_index("expert")
    all_flat = gathered_ids.reshape(experts, entry_count)
    matches = (all_flat == own_expert).astype(jnp.int32)
    ranked = jnp.cumsum(matches, axis=1) - matches
    sources = jnp.arange(experts, dtype=jnp.int32)[:, None]
    placed = jnp.where(matches == 1, sources * capacity + ranked, slot_total)
    entries = sources * entry_count + jnp.arange(entry_count, dtype=jnp.int32)[None, :]
    slot_table = (
        jnp.full((slot_total + 1,), experts * entry_count, jnp.int32)
        .at[placed.reshape(-1)]
        .set(entries.reshape(-1))[:slot_total]
    )
    token_of = slot_table // top_count
    received = jnp.concatenate([all_tokens, padding], axis=0)[token_of]
    output, pre_gate, pre_up = expert_forward(received, gate_matrix, up_matrix, down_matrix)
    slot_gates = jnp.concatenate([all_gates.reshape(-1), jnp.zeros((1,), jnp.float32)])[slot_table]
    chosen = jnp.concatenate([all_cotangent, padding], axis=0)[token_of]
    incoming = (slot_gates[:, None] * chosen.astype(jnp.float32)).astype(jnp.bfloat16)
    grad_rows = expert_backward(incoming, pre_gate, pre_up, gate_matrix, up_matrix, down_matrix)
    returned = lax.all_to_all(
        output.reshape(experts, capacity, model_width),
        "expert",
        split_axis=0,
        concat_axis=0,
        tiled=True,
    ).reshape(slot_total, model_width)
    returned_grads = lax.all_to_all(
        grad_rows.reshape(experts, capacity, model_width),
        "expert",
        split_axis=0,
        concat_axis=0,
        tiled=True,
    ).reshape(slot_total, model_width)
    picked = returned[places]
    weighted = flat_gates[:, None] * picked.astype(jnp.float32)
    mixed_rows = jnp.sum(weighted.reshape(row_count, top_count, model_width), axis=1).astype(
        jnp.bfloat16
    )
    gate_grads = jnp.einsum(
        "jd,jd->j", upstream, picked, preferred_element_type=jnp.float32
    ).reshape(row_count, top_count)
    picked_grads = returned_grads[places].astype(jnp.float32)
    row_grads = jnp.sum(picked_grads.reshape(row_count, top_count, model_width), axis=1).astype(
        jnp.bfloat16
    )
    return (mixed_rows, row_grads, gate_grads)


def solution(mesh):
    return jax.shard_map(
        local,
        mesh=mesh,
        in_specs=(
            P(("dp", "expert"), None),
            P(("dp", "expert"), None),
            P(("dp", "expert"), None),
            P("expert", None, None),
            P("expert", None, None),
            P("expert", None, None),
            P(("dp", "expert"), None),
        ),
        out_specs=(P(("dp", "expert"), None), P(("dp", "expert"), None), P(("dp", "expert"), None)),
        check_vma=False,
    )
```

profile of v0, /device:TPU:32, one launch (start us, length us, event | category | flops | bytes accessed | tf_op | source)
XLA Modules:
  0.0 932.4 jit_solution(493597241722205819)
XLA Ops:
  8.7 366.2 %all-gather = s32[128,16,8]{1,2,0:T(8,128)} all-gather(s32[1,16,8]{1,2,0:T(8,128)} %bitcast.48), channel_id=1, replica_groups=mesh['expert'=128,'dp'=2] {'expert'}, dimensions={0}, use_global_device_ids=true | all-gather | bytes 66048 | tf_op jit(solution)/shard_map/all_gather | solution.py:53
  374.9 1.2 copy.23
  376.1 1.4 copy.24
  377.5 1.7 reshape.152
  379.5 367.1 %all-gather.1 = f32[128,16,8]{1,2,0:T(8,128)} all-gather(f32[1,16,8]{1,2,0:T(8,128)S(1)} %bitcast.49), channel_id=1, replica_groups=mesh['expert'=128,'dp'=2] {'expert'}, dimensions={0}, use_global_device_ids=true | all-gather | bytes 66048 | tf_op jit(solution)/shard_map/all_gather | solution.py:54
  746.6 2.4 copy.28
  749.0 1.6 reshape.147
  751.0 60.3 %scatter_custom_fusion = s32[257]{0:T(512)S(1)} fusion(s32[16384]{0:T(1024)S(1)} %bitcast.47, s32[16384]{0:T(1024)S(1)} %add_bitcast_fusion, s32[]{:T(128)} %constant.19.clone.1), kind=kCustom, calls=%fused_computation.54 | custom fusion | bytes 1032 | tf_op jit(solution)/shard_map/scatter | solution.py:69
  811.3 1.9 gather_fusion.2
  813.3 8.3 concatenate.11
  821.5 7.8 gather_fusion.3
  829.3 8.3 concatenate.9
  837.6 7.9 gather_fusion
  845.5 3.3 fusion.10
  850.3 1.0 copy-done.7
  851.3 1.0 fusion
  852.4 1.0 fusion.4
  854.2 2.3 fusion.15
  856.5 2.5 reshape.148
  859.0 6.4 all-to-all-start.1
  865.5 4.4 fusion.18
  869.9 2.5 reshape.145
  872.4 14.2 %all-to-all-done.1 = bf16[128,2,2048]{2,1,0:T(2,128)(2,1)} async-done(((bf16[128,2,2048]{2,1,0:T(2,128)(2,1)}), bf16[128,2,2048]{2,1,0:T(2,128)(2,1)}, u32[]{:S(2)}, u32[]{:S(2)}) %all-to-all-start.1) | async-done | bytes 1048608 | tf_op jit(solution)/shard_map/all_to_all | solution.py:85
  886.6 7.7 all-to-all-start
  895.2 2.3 reshape.149
  897.4 3.6 gather_fusion.4
  901.0 2.0 bitcast_reduce_fusion
  903.0 12.6 %all-to-all-done = bf16[128,2,2048]{2,1,0:T(2,128)(2,1)} async-done(((bf16[128,2,2048]{2,1,0:T(2,128)(2,1)}), bf16[128,2,2048]{2,1,0:T(2,128)(2,1)}, u32[]{:S(2)}, u32[]{:S(2)}) %all-to-all-start) | async-done | bytes 1048608 | tf_op jit(solution)/shard_map/all_to_all | solution.py:78
  915.6 2.2 reshape.146
  917.8 3.6 gather_fusion.1
  921.4 1.3 fusion.22
  922.7 2.1 fusion.21
  (52 shorter events, 6.0 us)
Async XLA Ops:
  7.2 841.6 %copy-start = (bf16[1,2048,768]{2,1,0:T(8,128)(2,1)S(1)}, bf16[1,2048,768]{2,1,0:T(8,128)(2,1)}, u32[]{:S(2)}) copy-start(bf16[1,2048,768]{2,1,0:T(8,128)(2,1)} %param.11) | copy-start | bytes 9437188
  7.2 372.3 %copy-start.5 = (f32[16,8]{0,1:T(8,128)S(1)}, f32[16,8]{0,1:T(8,128)}, u32[]{:S(2)}) copy-start(f32[16,8]{0,1:T(8,128)} %param.9) | copy-start | bytes 1540
  7.2 806.1 %all-gather.7.cloned.1.call-start = ((), (), s32[]{:S(2)}) async-start(), calls=%async_computation.3 | async-start | bytes 8454144 | tf_op jit(solution)/shard_map/all_gather | solution.py:57
  7.9 821.4 %all-gather.5.cloned.1.call-start = ((), (), s32[]{:S(2)}) async-start(), calls=%async_computation.2 | async-start | bytes 8454144 | tf_op jit(solution)/shard_map/all_gather | solution.py:56
  845.5 3.3 copy-start.2
  848.8 4.6 copy-start.8
  848.8 1.5 copy-start.1
  848.8 2.5 copy-start.7
  851.3 2.1 copy-start.9
  852.3 1.9 copy-start.6
  859.0 27.5 %all-to-all-start.1 = ((bf16[128,2,2048]{2,1,0:T(2,128)(2,1)}), bf16[128,2,2048]{2,1,0:T(2,128)(2,1)}, u32[]{:S(2)}, u32[]{:S(2)}) async-start(bf16[128,2,2048]{2,1,0:T(2,128)(2,1)} %reshape.148), calls=%async_computation.1 | async-start | bytes 2097152 | tf_op jit(solution)/shard_map/all_to_all | solution.py:85
  869.9 24.4 %copy-start.4 = (s32[16,8]{0,1:T(8,128)S(1)}, s32[16,8]{0,1:T(8,128)}, u32[]{:S(2)}) copy-start(s32[16,8]{0,1:T(8,128)} %param.8) | copy-start | bytes 1540
  886.6 29.0 %all-to-all-start = ((bf16[128,2,2048]{2,1,0:T(2,128)(2,1)}), bf16[128,2,2048]{2,1,0:T(2,128)(2,1)}, u32[]{:S(2)}, u32[]{:S(2)}) async-start(bf16[128,2,2048]{2,1,0:T(2,128)(2,1)} %reshape.145), calls=%async_computation | async-start | bytes 2097152 | tf_op jit(solution)/shard_map/all_to_all | solution.py:78
  903.0 18.4 %copy-start.3 = (bf16[16,2048]{1,0:T(8,128)(2,1)S(1)}, bf16[16,2048]{1,0:T(8,128)(2,1)}, u32[]{:S(2)}) copy-start(bf16[16,2048]{1,0:T(8,128)(2,1)} %param.13) | copy-start | bytes 196612
Sparse Core Ops, SparseCore 0:
  11.6 126.3 all-gather.6
  141.6 121.2 all-gather.4
where the time goes:
time: 933 us; the launch traced here: 932 us
  blocking collectives  733 us (79%)
  local copies, waits for them, and re-layouts  123 us (13%)
  waiting for transfers between devices  28.1 us (3%)
  between operations  14.3 us (2%)
  starting transfers between devices  14.2 us (2%)
  matrix products  12.9 us (1%)
    all_gather x1, blocking collectives, local(): all_gates = lax.all_gather(gate_values, 'expert', axis=0, tiled=True)  367 us
    all_gather x1, blocking collectives, local(): gathered_ids = lax.all_gather(expert_ids, 'expert', axis=0, tiled=True)  366 us
    scatter x1, local copies, waits for them, and re-layouts, local(): slot_table = jnp.full((slot_total + 1,), experts * entry_count, jnp.int32...  60.3 us
  transfers between devices with their start and end apart: 4, of which 2 were waited for; matrix products, arithmetic and copies ran while one was open for 11% of the time, Pallas kernels for 0%

commit v1 on v0

--- a/solution.py
+++ b/solution.py
@@ -51,7 +51,12 @@
     upstream = jnp.repeat(cotangent, top_count, axis=0)
     padding = jnp.zeros((1, model_width), jnp.bfloat16)
     gathered_ids = lax.all_gather(expert_ids, "expert", axis=0, tiled=True)
-    all_gates = lax.all_gather(gate_values, "expert", axis=0, tiled=True)
+    all_gates = jnp.concatenate(
+        lax.all_to_all(
+            jnp.stack([gate_values for _ in range(lax.axis_size("expert"))]), "expert", 0, 0
+        ),
+        0,
+    )
     all_tokens, all_cotangent = (
         lax.all_gather(tokens, "expert", axis=0, tiled=True),
         lax.all_gather(cotangent, "expert", axis=0, tiled=True),

time: 933 us -> 591 us (0.63)
  blocking collectives: 733 us -> 364 us
  starting transfers between devices: 14.2 us -> 35.3 us
    all_gather x1 -> x0, blocking collectives: 367 us -> none  [local(): all_gates = lax.all_gather(gate_values, 'expert', axis=0, tiled=True)]
    all_to_all x0 -> x1, starting transfers between devices: none -> 15 us  [local(): lax.all_to_all(jnp.stack([gate_values for _ in range(lax.axis_size('exper...]
  transfers between devices with their start and end apart: 4 -> 5, of which waited for: 2 -> 2; matrix products, arithmetic and copies ran while one was open for 11% -> 18% of each run, Pallas kernels for 0% -> 0%
where the time goes in v1:
time: 591 us; the launch traced here: 590 us
  blocking collectives  364 us (62%)
  local copies, waits for them, and re-layouts  128 us (22%)
  starting transfers between devices  35.3 us (6%)
  waiting for transfers between devices  28.3 us (5%)
  between operations  14.4 us (2%)
  matrix products  12.9 us (2%)
  other arithmetic  7.13 us (1%)
    all_gather x1, blocking collectives, local(): gathered_ids = lax.all_gather(expert_ids, 'expert', axis=0, tiled=True)  364 us
    scatter x1, local copies, waits for them, and re-layouts, local(): slot_table = jnp.full((slot_total + 1,), experts * entry_count, jnp.int32...  60.3 us
    all_to_all x1, starting transfers between devices, local(): lax.all_to_all(jnp.stack([gate_values for _ in range(lax.axis_size('exper...  15 us
    all_to_all x1, waiting for transfers between devices, local(): lax.all_to_all(grad_rows.reshape(experts, capacity, model_width), 'expert...  14.3 us
    all_to_all x1, waiting for transfers between devices, local(): lax.all_to_all(output.reshape(experts, capacity, model_width), 'expert',...  12.5 us
    all_to_all x1, starting transfers between devices, local(): lax.all_to_all(grad_rows.reshape(experts, capacity, model_width), 'expert...  12.5 us
  transfers between devices with their start and end apart: 5, of which 2 were waited for; matrix products, arithmetic and copies ran while one was open for 18% of the time, Pallas kernels for 0%

profile of v1, /device:TPU:32, one launch (start us, length us, event | category | flops | bytes accessed | tf_op | source)
XLA Modules:
  0.0 590.4 jit_solution(17307392358107242303)
XLA Ops:
  8.7 1.5 broadcast_bitcast_fusion
  10.2 1.9 reshape.216
  12.1 15.0 %all-to-all-start.1 = ((f32[128,1,128]{2,1,0:T(1,128)}), f32[128,1,128]{2,1,0:T(1,128)S(1)}, u32[]{:S(2)}, u32[]{:S(2)}) async-start(f32[128,1,128]{2,1,0:T(1,128)} %reshape.216), calls=%async_computation.1 | async-start | bytes 131072 | tf_op jit(solution)/shard_map/all_to_all | solution.py:55
  27.1 364.2 %all-gather = s32[128,16,8]{1,2,0:T(8,128)} all-gather(s32[1,16,8]{1,2,0:T(8,128)} %bitcast.51), channel_id=1, replica_groups=mesh['expert'=128,'dp'=2] {'expert'}, dimensions={0}, use_global_device_ids=true | all-gather | bytes 66048 | tf_op jit(solution)/shard_map/all_gather | solution.py:53
  391.2 1.2 copy.24
  392.5 1.4 copy.25
  393.8 1.7 reshape.150
  396.2 60.3 %scatter_custom_fusion = s32[257]{0:T(512)S(1)} fusion(s32[16384]{0:T(1024)S(1)} %bitcast.50, s32[16384]{0:T(1024)S(1)} %add_bitcast_fusion, s32[]{:T(128)} %constant.19.clone.1), kind=kCustom, calls=%fused_computation.54 | custom fusion | bytes 1032 | tf_op jit(solution)/shard_map/scatter | solution.py:74
  458.9 2.4 copy.29
  461.3 1.6 reshape_reshape.3
  462.9 1.9 gather_fusion.2
  464.9 8.3 %concatenate.11 = bf16[2049,2048]{1,0:T(8,128)(2,1)} pad(bf16[2048,2048]{1,0:T(8,128)(2,1)} %all-gather.6.cloned.1.call-done, bf16[]{:T(256)} %constant.18.clone.1), padding=0_1x0_0 | pad | bytes 16781314 | tf_op jit(solution)/shard_map/concatenate | solution.py:80
  473.2 7.8 %gather_fusion.3 = bf16[256,2048]{1,0:T(8,128)(2,1)} fusion(bf16[2049,2048]{1,0:T(8,128)(2,1)} %concatenate.11, s32[1024]{0:T(1024)S(1)} %pad_clamp_fusion.2), kind=kCustom, calls=%fused_computation.3 | custom fusion | bytes 2098176 | tf_op jit(solution)/shard_map/gather | solution.py:80
  481.0 8.3 %concatenate.9 = bf16[2049,2048]{1,0:T(8,128)(2,1)} pad(bf16[2048,2048]{1,0:T(8,128)(2,1)} %all-gather.4.cloned.1.call-done, bf16[]{:T(256)} %constant.18.clone.1), padding=0_1x0_0 | pad | bytes 16781314 | tf_op jit(solution)/shard_map/concatenate | solution.py:77
  489.3 7.9 %gather_fusion = bf16[256,2048]{1,0:T(8,128)(2,1)} fusion(bf16[2049,2048]{1,0:T(8,128)(2,1)} %concatenate.9, s32[1024]{0:T(1024)S(1)} %pad_clamp_fusion.2), kind=kCustom, calls=%fused_computation | custom fusion | bytes 2098176 | tf_op jit(solution)/shard_map/gather | solution.py:77
  497.2 3.3 fusion.10
  502.9 1.0 fusion
  505.9 2.3 fusion.15
  508.2 2.5 reshape.146
  510.7 12.5 %all-to-all-start.2 = ((bf16[128,2,2048]{2,1,0:T(2,128)(2,1)}), bf16[128,2,2048]{2,1,0:T(2,128)(2,1)}, u32[]{:S(2)}, u32[]{:S(2)}) async-start(bf16[128,2,2048]{2,1,0:T(2,128)(2,1)} %reshape.146), calls=%async_computation.2 | async-start | bytes 2097152 | tf_op jit(solution)/shard_map/all_to_all | solution.py:90
  523.2 4.4 fusion.18
  527.6 2.6 reshape.144
  530.2 14.3 %all-to-all-done.2 = bf16[128,2,2048]{2,1,0:T(2,128)(2,1)} async-done(((bf16[128,2,2048]{2,1,0:T(2,128)(2,1)}), bf16[128,2,2048]{2,1,0:T(2,128)(2,1)}, u32[]{:S(2)}, u32[]{:S(2)}) %all-to-all-start.2) | async-done | bytes 1048608 | tf_op jit(solution)/shard_map/all_to_all | solution.py:90
  544.5 7.7 %all-to-all-start = ((bf16[128,2,2048]{2,1,0:T(2,128)(2,1)}), bf16[128,2,2048]{2,1,0:T(2,128)(2,1)}, u32[]{:S(2)}, u32[]{:S(2)}) async-start(bf16[128,2,2048]{2,1,0:T(2,128)(2,1)} %reshape.144), calls=%async_computation | async-start | bytes 2097152 | tf_op jit(solution)/shard_map/all_to_all | solution.py:83
  553.1 2.3 reshape.147
  555.3 3.6 gather_fusion.4
  558.9 2.0 bitcast_reduce_fusion
  561.0 12.5 %all-to-all-done = bf16[128,2,2048]{2,1,0:T(2,128)(2,1)} async-done(((bf16[128,2,2048]{2,1,0:T(2,128)(2,1)}), bf16[128,2,2048]{2,1,0:T(2,128)(2,1)}, u32[]{:S(2)}, u32[]{:S(2)}) %all-to-all-start) | async-done | bytes 1048608 | tf_op jit(solution)/shard_map/all_to_all | solution.py:83
  573.5 2.3 reshape.145
  575.8 3.6 gather_fusion.1
  579.4 1.3 fusion.22
  580.6 2.1 fusion.21
  (58 shorter events, 10.4 us)
Async XLA Ops:
  7.2 493.3 %copy-start = (bf16[1,2048,768]{2,1,0:T(8,128)(2,1)S(1)}, bf16[1,2048,768]{2,1,0:T(8,128)(2,1)}, u32[]{:S(2)}) copy-start(bf16[1,2048,768]{2,1,0:T(8,128)(2,1)} %param.11) | copy-start | bytes 9437188
  7.2 457.7 %all-gather.6.cloned.1.call-start = ((), (), s32[]{:S(2)}) async-start(), calls=%async_computation.4 | async-start | bytes 8454144 | tf_op jit(solution)/shard_map/all_gather | solution.py:62
  7.9 473.1 %all-gather.4.cloned.1.call-start = ((), (), s32[]{:S(2)}) async-start(), calls=%async_computation.3 | async-start | bytes 8454144 | tf_op jit(solution)/shard_map/all_gather | solution.py:61
  12.1 444.5 %all-to-all-start.1 = ((f32[128,1,128]{2,1,0:T(1,128)}), f32[128,1,128]{2,1,0:T(1,128)S(1)}, u32[]{:S(2)}, u32[]{:S(2)}) async-start(f32[128,1,128]{2,1,0:T(1,128)} %reshape.216), calls=%async_computation.1 | async-start | bytes 131072 | tf_op jit(solution)/shard_map/all_to_all | solution.py:55
  497.2 3.3 copy-start.2
  500.4 4.6 copy-start.8
  500.5 1.5 copy-start.1
  500.5 2.5 copy-start.7
  502.9 2.1 copy-start.9
  504.0 1.9 copy-start.6
  510.7 33.8 %all-to-all-start.2 = ((bf16[128,2,2048]{2,1,0:T(2,128)(2,1)}), bf16[128,2,2048]{2,1,0:T(2,128)(2,1)}, u32[]{:S(2)}, u32[]{:S(2)}) async-start(bf16[128,2,2048]{2,1,0:T(2,128)(2,1)} %reshape.146), calls=%async_computation.2 | async-start | bytes 2097152 | tf_op jit(solution)/shard_map/all_to_all | solution.py:90
  527.6 24.6 %copy-start.4 = (s32[16,8]{0,1:T(8,128)S(1)}, s32[16,8]{0,1:T(8,128)}, u32[]{:S(2)}) copy-start(s32[16,8]{0,1:T(8,128)} %param.8) | copy-start | bytes 1540
  527.6 24.7 %copy-start.5 = (f32[16,8]{0,1:T(8,128)S(1)}, f32[16,8]{0,1:T(8,128)}, u32[]{:S(2)}) copy-start(f32[16,8]{0,1:T(8,128)} %param.9) | copy-start | bytes 1540
  544.5 29.0 %all-to-all-start = ((bf16[128,2,2048]{2,1,0:T(2,128)(2,1)}), bf16[128,2,2048]{2,1,0:T(2,128)(2,1)}, u32[]{:S(2)}, u32[]{:S(2)}) async-start(bf16[128,2,2048]{2,1,0:T(2,128)(2,1)} %reshape.144), calls=%async_computation | async-start | bytes 2097152 | tf_op jit(solution)/shard_map/all_to_all | solution.py:83
  561.0 18.4 %copy-start.3 = (bf16[16,2048]{1,0:T(8,128)(2,1)S(1)}, bf16[16,2048]{1,0:T(8,128)(2,1)}, u32[]{:S(2)}) copy-start(bf16[16,2048]{1,0:T(8,128)(2,1)} %param.13) | copy-start | bytes 196612
Sparse Core Ops, SparseCore 0:
  11.6 126.3 all-gather.5
  141.6 121.1 all-gather.3
